TPU v7x, 32 devices: a whole 2x2x4 slice. The times are simulated.
32 devices in a mesh: ia: 2 (over y), ja: 4 (over x, core), ka: 4 (over z).
Axes of the slice: x: 2, y: 2, z: 4, core: 2. Of those that a mesh axis runs over, the one named last changes fastest.
Arguments:
- tensor: float32 [32, 256, 8192], P('ia', 'ka', 'ja'), may hold values from -6 to 6
- factor_b: float32 [8192, 64], P(('ja', 'ka')), may hold values from -1 to 1
- factor_c: float32 [256, 64], P('ka'), may hold values from -1 to 1
Outputs:
- factor_a: float32 [32, 64], P(('ia', 'ja', 'ka'))
- mode_two: float32 [64, 4, 2048], P(None, 'ja', ('ia', 'ka'))
All inputs are finite; a program needn't handle non-finite values.
Results may differ from a plain program's by a relative error of at most 0.00026.
Values sent between devices are 32-bit elements; how exact they have to be, the bound alone decides.
No kernel may reach another device: no remote copies, remote signals or barrier semaphores. Data moves between devices by JAX's collectives and lax.ppermute only.
A program may use at most 64 MiB of HBM per device.

v0:
```python
import jax
import jax.numpy as jnp
from jax import lax
from jax.sharding import PartitionSpec as P


def body(tensor, factor_b, factor_c):
    highest = lax.Precision.HIGHEST
    factor_rank = factor_c.shape[1]
    row_block = tensor.shape[0]
    column_block = tensor.shape[2]
    local_b = jnp.dot(factor_b.T, factor_b, precision=highest, preferred_element_type=jnp.float32)
    local_c = jnp.dot(factor_c.T, factor_c, precision=highest, preferred_element_type=jnp.float32)
    gram_b = lax.psum(local_b, ("ja", "ka"))
    gram_c = lax.psum(local_c, "ka")
    triangle = jnp.linalg.cholesky(gram_b * gram_c)
    partial_value = jnp.einsum("ikj,kr->rij", tensor, factor_c, precision=highest)
    mode_one = jnp.einsum(
        "rij,jr->ir",
        partial_value,
        lax.all_gather(factor_b, "ka", axis=0, tiled=True),
        precision=highest,
    )
    empty_two = jnp.zeros((factor_rank, column_block), jnp.float32)
    full_sum = lax.psum(mode_one, ("ja", "ka"))
    a_block = jax.scipy.linalg.cho_solve((triangle, True), full_sum.T).T
    row_count = row_block // (lax.axis_size("ja") * lax.axis_size("ka"))
    offset = (lax.axis_index("ja") * lax.axis_size("ka") + lax.axis_index("ka")) * row_count
    a_rows = lax.dynamic_slice_in_dim(a_block, offset, row_count, 0)
    contracted = jnp.einsum("ikj,kr->rij", tensor, factor_c, precision=highest)
    mode_partial = empty_two + jnp.einsum("rij,ir->rj", contracted, a_block, precision=highest)
    reduced = lax.psum_scatter(mode_partial, ("ia", "ka"), scatter_dimension=1, tiled=True)
    return (a_rows, reduced.reshape(factor_rank, 1, reduced.shape[1]))


def solution(mesh):
    placed = (P("ia", "ka", "ja"), P(("ja", "ka"), None), P("ka", None))
    return jax.shard_map(
        body,
        mesh=mesh,
        in_specs=placed,
        out_specs=(P(("ia", "ja", "ka"), None), P(None, "ja", ("ia", "ka"))),
        check_vma=False,
    )
```

profile of v0, /device:TPU:0, one launch (start us, length us, event | category | flops | bytes accessed | tf_op | source)
XLA Modules:
  0.0 229.5 jit_solution(2462762528005702529)
XLA Ops:
  7.2 0.0 copy-start
  7.2 0.0 reduce-scatter.2.cloned.1.call-start
  7.2 17.6 %all_gather.3 = f32[2048,64]{0,1:T(8,128)S(1)} all-gather(f32[512,64]{0,1:T(8,128)} %param.4), channel_id=1, replica_groups=mesh['ia'=2,'ja'=4,'ka'=4] {'ka'}, dimensions={0}, use_global_device_ids=true | all-gather | bytes 655360 | tf_op jit(solution)/shard_map/all_gather | solution.py:21
  24.8 1.2 fusion.13
  26.1 0.0 copy-done
  26.1 0.2 fusion.14
  26.3 11.6 %fusion.6 = f32[64,16,2048]{2,0,1:T(8,128)} fusion(f32[16,64,2048]{2,1,0:T(8,128)} %param.3, f32[64,64]{1,0:T(8,128)S(1)} %copy-done), kind=kOutput, calls=%fused_computation.8 | convolution fusion | flops 1610612736 | bytes 16793600 | tf_op jit(solution)/shard_map/ikj,kr->rij/dot_general | solution.py:17
  37.9 19.8 %psum.22 = f32[64,64]{0,1:T(8,128)S(1)} all-reduce(f32[64,64]{0,1:T(8,128)S(1)} %fusion.14), channel_id=1, replica_groups=mesh['ia'=2,'ja'=4,'ka'=4] {'ka'}, use_global_device_ids=true, to_apply=%region_1.0 | all-reduce | flops 4096 | bytes 32768 | tf_op jit(solution)/shard_map/psum | solution.py:15
  57.7 17.9 %fusion.2 = f32[64,1,16]{2,1,0:T(1,128)S(1)} fusion(f32[64,16,2048]{2,0,1:T(8,128)} %fusion.6, f32[2048,64,1]{0,1,2:T(8,128)S(1)} %bitcast.31), kind=kOutput, calls=%fused_computation.2 | convolution fusion | flops 25165824 | bytes 8916992 | tf_op jit(solution)/shard_map/rij,jr->ir/dot_general | solution.py:18
  75.6 58.2 %all-reduce = (f32[16,64]{0,1:T(8,128)S(1)}, f32[64,64]{0,1:T(8,128)S(1)}) all-reduce(f32[16,64]{0,1:T(8,128)S(1)} %bitcast.33, f32[64,64]{0,1:T(8,128)S(1)} %fusion.13), channel_id=1, replica_groups=mesh['ia'=2,'ja'=4,'ka'=4] {'ja','ka'}, use_global_device_ids=true, to_apply=%region_4.5 | all-reduce | flops 5120 | bytes 40960 | tf_op jit(solution)/shard_map/psum | solution.py:25
  133.8 0.1 copy.7
  133.9 5.8 %cholesky.16 = f32[64,64]{1,0:T(8,128)S(1)} custom-call(f32[64,64]{1,0:T(8,128)S(1)} %fusion.12), custom_call_target="Cholesky" | custom-call | tf_op jit(solution)/shard_map/jit(cholesky)/cholesky | solution.py:16
  139.7 0.6 compare_reduce_fusion
  140.4 0.7 fusion.5
  141.0 4.9 %custom-call.10 = f32[1,64,64]{1,2,0:T(8,128)S(1)} custom-call(f32[1,64,64]{2,1,0:T(8,128)S(1)} %fusion.5), custom_call_target="InvertDiagBlocksLowerTriangular" | custom-call | tf_op jit(solution)/shard_map/jit(_cho_solve)/triangular_solve | solution.py:26
  145.9 0.3 fusion.10
  146.2 0.2 fusion.8
  146.4 0.1 copy.15
  146.5 12.3 %fusion = f32[64,1,2048]{2,1,0:T(1,128)S(1)} fusion(f32[16,64,1]{0,2,1:T(1,128)S(1)} %copy.15, f32[64,16,2048]{2,0,1:T(8,128)} %fusion.6), kind=kOutput, calls=%fused_computation | convolution fusion | flops 25165824 | bytes 8916992 | tf_op jit(solution)/shard_map/rij,ir->rj/dot_general | solution.py:31
  158.8 1.0 copy.25
  159.8 0.0 reduce-scatter.2.cloned.1.call-update
  159.8 0.5 constant_dynamic-slice_fusion
  160.3 60.9 %reduce-scatter.2.cloned.1.call-done = f32[64,256]{1,0:T(8,128)} async-done(((f32[64,2048]{1,0:T(8,128)}), f32[64,256]{1,0:T(8,128)}) %reduce-scatter.2.cloned.1.call-update) | async-done | bytes 65552 | tf_op jit(solution)/shard_map/reduce_scatter | solution.py:32
  221.2 1.5 reshape.20
  (3 shorter events, 0.0 us)
Async XLA Ops:
  7.2 18.9 %copy-start = (f32[64,64]{1,0:T(8,128)S(1)}, f32[64,64]{1,0:T(8,128)}, u32[]{:S(2)}) copy-start(f32[64,64]{1,0:T(8,128)} %param.5) | copy-start | bytes 49156
  7.2 214.0 %reduce-scatter.2.cloned.1.call-start = ((), (), s32[]{:S(2)}) async-start(), calls=%async_computation.1 | async-start | bytes 589824 | tf_op jit(solution)/shard_map/reduce_scatter | solution.py:32
Sparse Core Ops, SparseCore 0:
  159.9 61.2 reduce-scatter.1
where the time goes:
time: 230 us
  blocking collectives  95.6 us (42%)
  waiting for transfers between devices  60.9 us (26%)
  matrix products  43.7 us (19%)
  between operations  14.1 us (6%)
  other arithmetic  12.1 us (5%)
  local copies, waits for them, and re-layouts  3.15 us (1%)
    reduce_scatter x1, waiting for transfers between devices, body(): lax.psum_scatter(mode_partial, ('ia', 'ka'), scatter_dimension=1, tiled=T...  60.9 us
    psum x1, blocking collectives, body(): full_sum = lax.psum(mode_one, ('ja', 'ka'))  58.2 us
    psum x1, blocking collectives, body(): gram_c = lax.psum(local_c, 'ka')  19.8 us
    dot_general x1, matrix products, body(): jnp.einsum('rij,jr->ir', partial_value, lax.all_gather(factor_b, 'ka', ax...  17.9 us
    all_gather x1, blocking collectives, body(): lax.all_gather(factor_b, 'ka', axis=0, tiled=True)  17.6 us
    dot_general x1, matrix products, body(): jnp.einsum('rij,ir->rj', contracted, a_block, precision=highest)  12.3 us
    dot_general x1, matrix products, body(): jnp.einsum('ikj,kr->rij', tensor, factor_c, precision=highest)  11.6 us
    another operation x3, other arithmetic, body(): triangle = jnp.linalg.cholesky(gram_b * gram_c)  6.52 us
  transfers between devices with their start and end apart: 1, of which 1 were waited for; matrix products, arithmetic and copies ran while one was open for 0% of the time, Pallas kernels for 0%

commit v1 on v0

--- a/solution.py
+++ b/solution.py
@@ -15,11 +15,35 @@
     gram_c = lax.psum(local_c, "ka")
     triangle = jnp.linalg.cholesky(gram_b * gram_c)
     partial_value = jnp.einsum("ikj,kr->rij", tensor, factor_c, precision=highest)
-    mode_one = jnp.einsum(
-        "rij,jr->ir",
-        partial_value,
-        lax.all_gather(factor_b, "ka", axis=0, tiled=True),
-        precision=highest,
+
+    def keep_up_page(frame, peer_axis, tile_in):
+        arr_now, f_next, finding = (
+            lax.axis_size(peer_axis),
+            lax.axis_index(peer_axis),
+            frame.shape[0],
+        )
+        table = [(ii, (ii + 1) % arr_now) for ii in range(arr_now)]
+        m_next, plain = (frame, None)
+        for hop_no in [*range(arr_now)]:
+            a_now = (
+                lax.ppermute(m_next, axis_name=peer_axis, perm=table)
+                if hop_no < arr_now - 1
+                else None
+            )
+            out_arr = tile_in(m_next, (f_next - hop_no) % arr_now * finding)
+            plain = out_arr if plain is None else plain + out_arr
+            m_next = a_now
+        return plain
+
+    mode_one = keep_up_page(
+        factor_b,
+        "ka",
+        lambda part, start: jnp.einsum(
+            "rij,jr->ir",
+            lax.dynamic_slice_in_dim(partial_value, start, part.shape[0], axis=2),
+            part,
+            precision=highest,
+        ),
     )
     empty_two = jnp.zeros((factor_rank, column_block), jnp.float32)
     full_sum = lax.psum(mode_one, ("ja", "ka"))

time: 230 us -> 221 us (0.961)
  blocking collectives: 95.6 us -> 76.5 us
  waiting for transfers between devices: 60.9 us -> 67.7 us
  local copies, waits for them, and re-layouts: 3.15 us -> 7.75 us
  matrix products: 43.7 us -> 39.4 us
  starting transfers between devices: 0.04 us -> 3.38 us
    all_gather x1 -> x0, blocking collectives: 17.6 us -> none  [body(): lax.all_gather(factor_b, 'ka', axis=0, tiled=True)]
    ppermute x0 -> x3, waiting for transfers between devices: none -> 6.83 us  [keep_up_page(): lax.ppermute(m_next, axis_name=peer_axis, perm=table)]
    dynamic_slice x0 -> x1, local copies, waits for them, and re-layouts: none -> 4.59 us  [body(): lax.dynamic_slice_in_dim(partial_value, start, part.shape[0], axis=2)]
    ppermute x0 -> x3, starting transfers between devices: none -> 3.35 us  [keep_up_page(): lax.ppermute(m_next, axis_name=peer_axis, perm=table)]
    dot_general x1 -> x4, matrix products: 17.9 us -> 14.6 us  [body(): jnp.einsum('rij,jr->ir', lax.dynamic_slice_in_dim(partial_value, start, p...]
  transfers between devices with their start and end apart: 1 -> 4, of which waited for: 1 -> 3; matrix products, arithmetic and copies ran while one was open for 0% -> 13% of each run, Pallas kernels for 0% -> 0%
where the time goes in v1:
time: 221 us
  blocking collectives  76.5 us (35%)
  waiting for transfers between devices  67.7 us (31%)
  matrix products  39.4 us (18%)
  between operations  14.2 us (6%)
  other arithmetic  12.1 us (5%)
  local copies, waits for them, and re-layouts  7.75 us (4%)
  starting transfers between devices  3.38 us (2%)
    reduce_scatter x1, waiting for transfers between devices, body(): lax.psum_scatter(mode_partial, ('ia', 'ka'), scatter_dimension=1, tiled=T...  60.8 us
    psum x1, blocking collectives, body(): full_sum = lax.psum(mode_one, ('ja', 'ka'))  58.2 us
    psum x1, blocking collectives, body(): gram_c = lax.psum(local_c, 'ka')  18.3 us
    dot_general x4, matrix products, body(): jnp.einsum('rij,jr->ir', lax.dynamic_slice_in_dim(partial_value, start, p...  14.6 us
    dot_general x1, matrix products, body(): jnp.einsum('rij,ir->rj', contracted, a_block, precision=highest)  12.3 us
    dot_general x1, matrix products, body(): jnp.einsum('ikj,kr->rij', tensor, factor_c, precision=highest)  11.6 us
    ppermute x3, waiting for transfers between devices, keep_up_page(): lax.ppermute(m_next, axis_name=peer_axis, perm=table)  6.83 us
    another operation x3, other arithmetic, body(): triangle = jnp.linalg.cholesky(gram_b * gram_c)  6.52 us
  transfers between devices with their start and end apart: 4, of which 3 were waited for; matrix products, arithmetic and copies ran while one was open for 13% of the time, Pallas kernels for 0%

profile of v1, /device:TPU:0, one launch (start us, length us, event | category | flops | bytes accessed | tf_op | source)
XLA Modules:
  0.0 221.1 jit_solution(8345812106440013657)
XLA Ops:
  7.2 3.1 %collective-permute-start = (f32[512,64]{0,1:T(8,128)}, f32[512,64]{0,1:T(8,128)S(1)}, u32[]{:S(2)}, u32[]{:S(2)}) collective-permute-start(f32[512,64]{0,1:T(8,128)} %param.4), channel_id=1, source_target_pairs={{0,1},{1,2},{2,3},{3,0},{4,5},{5,6},{6,7},{7,4},{8,9},{9,10},{10,1... | collective-permute-start | bytes 393224 | tf_op jit(solution)/shard_map/ppermute | solution.py:29
  10.3 0.2 fusion.23
  10.6 11.6 %fusion.15 = f32[64,16,2048]{2,0,1:T(8,128)} fusion(f32[16,64,2048]{2,1,0:T(8,128)} %param.3, f32[64,64]{1,0:T(8,128)S(1)} %copy-done), kind=kOutput, calls=%fused_computation.17 | convolution fusion | flops 1610612736 | bytes 16793600 | tf_op jit(solution)/shard_map/ikj,kr->rij/dot_general | solution.py:17
  22.1 18.3 %psum.22 = f32[64,64]{0,1:T(8,128)S(1)} all-reduce(f32[64,64]{0,1:T(8,128)S(1)} %fusion.23), channel_id=1, replica_groups=mesh['ia'=2,'ja'=4,'ka'=4] {'ka'}, use_global_device_ids=true, to_apply=%region_1.0 | all-reduce | flops 4096 | bytes 32768 | tf_op jit(solution)/shard_map/psum | solution.py:15
  40.5 4.6 %constant_dynamic-slice_fusion.3 = (f32[64,16,512]{2,0,1:T(8,128)S(1)}, f32[64,16,512]{2,0,1:T(8,128)S(1)}, f32[64,16,512]{2,0,1:T(8,128)S(1)}, f32[64,16,512]{2,0,1:T(8,128)S(1)}) fusion(f32[64,16,2048]{2,0,1:T(8,128)} %fusion.15, s32[]{:T(128)S(6)} %select_n.42, s32[]{:T(128)S(6)} %select_n.46, s32[]{:T(128)S(6)} %select_n.44, s32[]{:T(128)S(6)} %select_n.40), kind=kLoop, calls=%fused_computation.33 | loop fusion | bytes 16777232 | tf_op jit(solution)/shard_map/dynamic_slice | solution.py:43
  45.1 3.6 %fusion.8 = f32[64,1,16]{2,1,0:T(1,128)S(1)} fusion(f32[64,16,512]{2,0,1:T(8,128)S(1)} %get-tuple-element.7, f32[512,64,1]{0,1,2:T(8,128)S(1)} %bitcast.41), kind=kOutput, calls=%fused_computation.8 | convolution fusion | flops 6291456 | bytes 2232320 | tf_op jit(solution)/shard_map/rij,jr->ir/dot_general | solution.py:41
  48.8 0.3 fusion.22
  49.0 0.2 collective-permute-start.1
  49.3 3.6 %fusion.6 = f32[64,1,16]{2,1,0:T(1,128)S(1)} fusion(f32[64,16,512]{2,0,1:T(8,128)S(1)} %get-tuple-element.4, f32[512,64,1]{0,1,2:T(8,128)S(1)} %bitcast.46), kind=kOutput, calls=%fused_computation.6 | convolution fusion | flops 6291456 | bytes 2232320 | tf_op jit(solution)/shard_map/rij,jr->ir/dot_general | solution.py:41
  52.9 3.7 %collective-permute-done.1 = f32[512,64]{0,1:T(8,128)S(1)} collective-permute-done((f32[512,64]{0,1:T(8,128)S(1)}, f32[512,64]{0,1:T(8,128)S(1)}, u32[]{:S(2)}, u32[]{:S(2)}) %collective-permute-start.1) | collective-permute-done | bytes 131104 | tf_op jit(solution)/shard_map/ppermute | solution.py:29
  56.6 3.6 %fusion.4 = f32[64,1,16]{2,1,0:T(1,128)S(1)} fusion(f32[64,16,512]{2,0,1:T(8,128)S(1)} %get-tuple-element.6, f32[512,64,1]{0,1,2:T(8,128)S(1)} %bitcast.47), kind=kOutput, calls=%fused_computation.4 | convolution fusion | flops 6291456 | bytes 2232320 | tf_op jit(solution)/shard_map/rij,jr->ir/dot_general | solution.py:41
  60.3 3.1 %collective-permute-done.2 = f32[512,64]{0,1:T(8,128)S(1)} collective-permute-done((f32[512,64]{0,1:T(8,128)S(1)}, f32[512,64]{0,1:T(8,128)S(1)}, u32[]{:S(2)}, u32[]{:S(2)}) %collective-permute-start.2) | collective-permute-done | bytes 131104 | tf_op jit(solution)/shard_map/ppermute | solution.py:29
  63.4 3.6 %fusion.2 = f32[64,1,16]{2,1,0:T(1,128)S(1)} fusion(f32[64,16,512]{2,0,1:T(8,128)S(1)} %get-tuple-element.5, f32[512,64,1]{0,1,2:T(8,128)S(1)} %bitcast.48), kind=kOutput, calls=%fused_computation.2 | convolution fusion | flops 6291456 | bytes 2232320 | tf_op jit(solution)/shard_map/rij,jr->ir/dot_general | solution.py:41
  67.1 58.2 %all-reduce = (f32[16,64]{0,1:T(8,128)S(1)}, f32[64,64]{0,1:T(8,128)S(1)}) all-reduce(f32[16,64]{0,1:T(8,128)S(1)} %add_bitcast_fusion, f32[64,64]{0,1:T(8,128)S(1)} %fusion.22), channel_id=1, replica_groups=mesh['ia'=2,'ja'=4,'ka'=4] {'ja','ka'}, use_global_device_ids=true, to_apply=%region_4.5 | all-reduce | flops 5120 | bytes 40960 | tf_op jit(solution)/shard_map/psum | solution.py:49
  125.4 5.8 %cholesky.16 = f32[64,64]{1,0:T(8,128)S(1)} custom-call(f32[64,64]{1,0:T(8,128)S(1)} %fusion.21), custom_call_target="Cholesky" | custom-call | tf_op jit(solution)/shard_map/jit(cholesky)/cholesky | solution.py:16
  131.3 0.6 compare_reduce_fusion
  131.9 0.7 fusion.14
  132.6 4.9 %custom-call.10 = f32[1,64,64]{1,2,0:T(8,128)S(1)} custom-call(f32[1,64,64]{2,1,0:T(8,128)S(1)} %fusion.14), custom_call_target="InvertDiagBlocksLowerTriangular" | custom-call | tf_op jit(solution)/shard_map/jit(_cho_solve)/triangular_solve | solution.py:50
  137.5 0.3 fusion.19
  138.0 12.3 %fusion = f32[64,1,2048]{2,1,0:T(1,128)S(1)} fusion(f32[16,64,1]{0,2,1:T(1,128)S(1)} %copy.25, f32[64,16,2048]{2,0,1:T(8,128)} %fusion.15), kind=kOutput, calls=%fused_computation | convolution fusion | flops 25165824 | bytes 8916992 | tf_op jit(solution)/shard_map/rij,ir->rj/dot_general | solution.py:55
  150.4 1.0 copy.47
  151.4 0.5 constant_dynamic-slice_fusion
  151.9 60.8 %reduce-scatter.2.cloned.1.call-done = f32[64,256]{1,0:T(8,128)} async-done(((f32[64,2048]{1,0:T(8,128)}), f32[64,256]{1,0:T(8,128)}) %reduce-scatter.2.cloned.1.call-update) | async-done | bytes 65552 | tf_op jit(solution)/shard_map/reduce_scatter | solution.py:56
  212.7 1.5 reshape.20
  (15 shorter events, 0.5 us)
Async XLA Ops:
  7.2 3.2 %copy-start = (f32[64,64]{1,0:T(8,128)S(1)}, f32[64,64]{1,0:T(8,128)}, u32[]{:S(2)}) copy-start(f32[64,64]{1,0:T(8,128)} %param.5) | copy-start | bytes 49156
  7.2 205.5 %reduce-scatter.2.cloned.1.call-start = ((), (), s32[]{:S(2)}) async-start(), calls=%async_computation.1 | async-start | bytes 589824 | tf_op jit(solution)/shard_map/reduce_scatter | solution.py:56
  7.2 41.8 %collective-permute-start = (f32[512,64]{0,1:T(8,128)}, f32[512,64]{0,1:T(8,128)S(1)}, u32[]{:S(2)}, u32[]{:S(2)}) collective-permute-start(f32[512,64]{0,1:T(8,128)} %param.4), channel_id=1, source_target_pairs={{0,1},{1,2},{2,3},{3,0},{4,5},{5,6},{6,7},{7,4},{8,9},{9,10},{10,1... | collective-permute-start | bytes 393224 | tf_op jit(solution)/shard_map/ppermute | solution.py:29
  40.5 4.6 %copy-start.1 = (f32[512,64]{0,1:T(8,128)S(1)}, f32[512,64]{0,1:T(8,128)}, u32[]{:S(2)}) copy-start(f32[512,64]{0,1:T(8,128)} %param.4) | copy-start | bytes 393220
  49.0 7.6 %collective-permute-start.1 = (f32[512,64]{0,1:T(8,128)S(1)}, f32[512,64]{0,1:T(8,128)S(1)}, u32[]{:S(2)}, u32[]{:S(2)}) collective-permute-start(f32[512,64]{0,1:T(8,128)S(1)} %collective-permute-done), channel_id=1, source_target_pairs={{0,1},{1,2},{2,3},{3,0},{4,5},{5,6},{6,7},{7,4},{8,9},{9,10},{10,1... | collective-permute-start | bytes 393224 | tf_op jit(solution)/shard_map/ppermute | solution.py:29
  56.6 6.8 %collective-permute-start.2 = (f32[512,64]{0,1:T(8,128)S(1)}, f32[512,64]{0,1:T(8,128)S(1)}, u32[]{:S(2)}, u32[]{:S(2)}) collective-permute-start(f32[512,64]{0,1:T(8,128)S(1)} %collective-permute-done.1), channel_id=1, source_target_pairs={{0,1},{1,2},{2,3},{3,0},{4,5},{5,6},{6,7},{7,4},{8,9},{9,10},{10,1... | collective-permute-start | bytes 393224 | tf_op jit(solution)/shard_map/ppermute | solution.py:29
Sparse Core Ops, SparseCore 0:
  151.5 61.1 reduce-scatter.1
